TPU v7x, 32 devices: a whole 2x2x4 slice. The times are simulated.
32 devices in a mesh: grid: 4 (over z), basis: 8 (over y, x, core).
Axes of the slice: x: 2, y: 2, z: 4, core: 2. Of those that a mesh axis runs over, the one named last changes fastest.
Arguments:
- basis_values: bfloat16 [512, 256, 512], P(('grid', 'basis')), may hold values from -6 to 6
- weights: float32 [512, 256], P(('grid', 'basis')), may hold values from 0.1 to 1
- points: bfloat16 [512, 3, 256], P(('grid', 'basis')), may hold values from 0 to 1
- block_lists: int32 [512, 4], P(('grid', 'basis')), may hold values from 0 to 31, as said below
- counts: int32 [8, 4], P('basis', 'grid'), may hold values from 1 to 16, 32 in all within a row
- density: bfloat16 [4096, 4096], P('basis'), may hold values from -0.25 to 0.25
- centers: float32 [3, 4096], replicated, may hold values from 0 to 1
- block_centers: float32 [3, 32], replicated, may hold values from 0 to 1
- block_exponents: float32 [32], replicated, may hold values from 2 to 20
Outputs:
- exchange_matrix: float32 [4096, 4096], P('basis', 'grid')
Inputs may be any that keep to these rules, and one draw needn't show every extreme that they name: `block_lists`: each row names 4 different blocks. The rows of all devices with the same basis index name together exactly 8 different blocks, consecutive ones counted on from 31 to 0, and the rows of each such device name all 8 of them; one of them is named by every row of those devices. The blocks of basis index 0 begin at block 31. Entry [b, g] counts the live batches of the device at grid index g and basis index b, which are its first ones. Each row sums to 32 and its largest entry is 16.
All inputs are finite; a program needn't handle non-finite values.
Results may differ from a plain program's by a relative error of at most 0.0018.
Values may be sent and summed in bfloat16 or wider, within the bound.
A program may use at most 128 MiB of HBM per device.

v0:
```python
import functools
import math

import jax
import jax.numpy as jnp
from jax import lax
from jax.experimental import pallas as pl
from jax.experimental.pallas import tpu as pltpu
from jax.sharding import PartitionSpec as P

TB = 128
CL = 8


def boys_table(points_f, blocks, block_centers, block_exponents):
    centre = block_centers[:, blocks]
    middle = 0.5 * (centre[:, :, :, None] + centre[:, :, None, :])
    exponents = block_exponents[blocks]
    rate_pair = 0.5 * (exponents[:, :, None] + exponents[:, None, :])
    offset = points_f.transpose(1, 0, 2)[:, :, None, None, :] - middle[:, :, :, :, None]
    distance = jnp.sum(offset * offset, axis=0)
    tau_value = rate_pair[:, :, :, None] * distance + 0.05
    root_value = jnp.sqrt(tau_value)
    return 0.5 * math.sqrt(math.pi) * lax.erf(root_value) / root_value


def first_block_of(block_lists, block_count):
    present = jnp.any(
        block_lists.reshape(-1)[:, None] == jnp.arange(block_count, dtype=jnp.int32)[None, :],
        axis=0,
    )
    begins = present & jnp.logical_not(jnp.roll(present, 1))
    return jnp.sum(jnp.where(begins, jnp.arange(block_count, dtype=jnp.int32), 0))


def block_with_residue(first, residue, block_count):
    return (first + (residue - first) % CL) % block_count


def region_coupling(members, centers):
    functions = (members[:, None] * TB + jnp.arange(TB, dtype=jnp.int32)[None, :]).reshape(CL * TB)
    where_at = centers[:, functions].reshape(3, CL, TB)
    spread = where_at[:, :, None, :, None] - where_at[:, None, :, None, :]
    distance = jnp.sum(spread * spread, axis=0)
    sharpness = float(centers.shape[1]) ** (2.0 / 3.0)
    return jnp.exp(-sharpness * distance).astype(jnp.bfloat16)


def pack_kernel(column_ref, dens_ref, out_ref, sems):
    targets, per = out_ref.shape[:2]

    def copy(t, c):
        at = pl.multiple_of(column_ref[t, c] * TB, TB)
        return pltpu.make_async_copy(
            dens_ref.at[:, pl.ds(at, TB)], out_ref.at[t, c], sems.at[t, c]
        )

    for c in range(per):
        for t in range(targets):
            copy(t, c).start()
    for c in range(per):
        for t in range(targets):
            copy(t, c).wait()


def pack_density(columns, density):
    targets, per = columns.shape
    rows = density.shape[0]
    return pl.pallas_call(
        pack_kernel,
        in_specs=[
            pl.BlockSpec(memory_space=pltpu.SMEM),
            pl.BlockSpec(memory_space=pl.ANY),
        ],
        out_specs=pl.BlockSpec(memory_space=pltpu.VMEM),
        out_shape=jax.ShapeDtypeStruct((targets, per, rows, TB), jnp.bfloat16),
        scratch_shapes=[pltpu.SemaphoreType.DMA((targets, per))],
        name="pack_density",
    )(columns, density)


def fetch_kernel(grid_size, basis_size, owned, slot_ref, packed, out, *scratch):
    per = CL // grid_size
    landed = scratch[:per]
    x_send, x_recv, z_send, z_recv = scratch[per:]
    me_grid = lax.axis_index("grid")
    me_basis = lax.axis_index("basis")
    mesh_ids = pl.DeviceIdType.MESH

    barrier = pltpu.get_barrier_semaphore()
    for d in (1, grid_size - 1):
        pl.semaphore_signal(
            barrier,
            inc=1,
            device_id=(lax.rem(me_grid + d, grid_size), me_basis),
            device_id_type=mesh_ids,
        )
    for d in range(1, basis_size):
        pl.semaphore_signal(
            barrier,
            inc=1,
            device_id=(me_grid, lax.rem(me_basis + d, basis_size)),
            device_id_type=mesh_ids,
        )
    pl.semaphore_wait(barrier, basis_size + 1)

    def x_copy(cc, d):
        to = lax.rem(me_basis + d, basis_size)
        return pltpu.make_async_remote_copy(
            src_ref=packed.at[to, cc],
            dst_ref=landed[cc].at[d],
            send_sem=x_send.at[d - 1, cc],
            recv_sem=x_recv.at[d - 1, cc],
            device_id=(me_grid, to),
            device_id_type=mesh_ids,
        )

    def z_copy(cc, j, side):
        step = 1 if side == 0 else grid_size - 1
        return pltpu.make_async_remote_copy(
            src_ref=out.at[j, cc],
            dst_ref=out.at[j, cc],
            send_sem=z_send.at[j, cc, side],
            recv_sem=z_recv.at[j, cc],
            device_id=(lax.rem(me_grid + step, grid_size), me_basis),
            device_id_type=mesh_ids,
        )

    def own(cc):
        landed[cc][0] = packed[me_basis, cc]
        for d in range(1, basis_size):
            x_copy(cc, d).wait_recv()
        for r in range(CL):
            out[me_grid, cc, r] = landed[cc][
                slot_ref[r], (r % owned) * TB : (r % owned + 1) * TB, :
            ]

        @pl.when(me_grid < grid_size - 1)
        def _():
            z_copy(cc, me_grid, 0).start()

        @pl.when(me_grid > 0)
        def _():
            z_copy(cc, me_grid, 1).start()

    def relay(cc, h):
        @pl.when(me_grid >= h)
        def _():
            z_copy(cc, me_grid - h, 0).wait_recv()

            @pl.when(me_grid < grid_size - 1)
            def _():
                z_copy(cc, me_grid - h, 0).start()

        @pl.when(me_grid + h < grid_size)
        def _():
            z_copy(cc, me_grid + h, 1).wait_recv()

            @pl.when(me_grid > 0)
            def _():
                z_copy(cc, me_grid + h, 1).start()

    for cc in range(per):
        for d in range(1, basis_size):
            x_copy(cc, d).start()
    for cc in range(per):
        own(cc)
        if grid_size > 1:
            relay(cc, 1)
    for h in range(2, grid_size):
        for cc in range(per):
            relay(cc, h)

    for cc in range(per):
        for d in range(1, basis_size):
            x_copy(cc, d).wait_send()
        for h in range(grid_size):

            @pl.when((me_grid >= h) & (me_grid < grid_size - 1))
            def _():
                z_copy(cc, me_grid - h, 0).wait_send()

            @pl.when((me_grid + h < grid_size) & (me_grid > 0))
            def _():
                z_copy(cc, me_grid + h, 1).wait_send()


def fetch_density(slots, packed, grid_size, basis_size, owned):
    per = CL // grid_size
    vmem = pl.BlockSpec(memory_space=pltpu.VMEM)
    return pl.pallas_call(
        functools.partial(fetch_kernel, grid_size, basis_size, owned),
        out_shape=jax.ShapeDtypeStruct((grid_size, per, CL, TB, TB), jnp.bfloat16),
        in_specs=[pl.BlockSpec(memory_space=pltpu.SMEM), vmem],
        out_specs=vmem,
        scratch_shapes=[pltpu.VMEM((basis_size, owned * TB, TB), jnp.bfloat16)] * per
        + [
            pltpu.SemaphoreType.DMA((basis_size - 1, per)),
            pltpu.SemaphoreType.DMA((basis_size - 1, per)),
            pltpu.SemaphoreType.DMA((grid_size, per, 2)),
            pltpu.SemaphoreType.DMA((grid_size, per)),
        ],
        compiler_params=pltpu.CompilerParams(
            collective_id=1, has_side_effects=True, vmem_limit_bytes=32 * 1024 * 1024
        ),
        name="fetch_density",
    )(slots, packed)


def encode(tile):
    top = jnp.maximum(jnp.max(jnp.abs(tile), axis=0, keepdims=True), 1e-30)
    steps = jnp.round(tile * (32767.0 / top))
    return steps.astype(jnp.int32).astype(jnp.int16), top * (1.0 / 32767.0)


def decode(coded, scale):
    return coded.astype(jnp.int32).astype(jnp.float32) * scale


def batch_kernel(
    per, place_ref, count_ref, values_ref, weighted_ref, boys_ref, dens_ref, coup_ref, out_ref, scale_ref, acc
):
    n = pl.program_id(0)
    lists = place_ref.shape[1]

    @pl.when(n == 0)
    def _():
        acc[...] = jnp.zeros_like(acc)

    @pl.when(n < count_ref[0])
    def _():
        at = [place_ref[n, t] for t in range(lists)]
        dens = jnp.concatenate(
            [
                jnp.concatenate([dens_ref[c // per, c % per, r] for c in at], axis=1)
                for r in at
            ],
            axis=0,
        )
        mapped = lax.dot_general(
            dens, values_ref[0], (((1,), (1,)), ((), ())), preferred_element_type=jnp.float32
        ).astype(jnp.bfloat16)
        total = None
        for u in range(lists):
            coup = jnp.concatenate([coup_ref[r, at[u]] for r in at], axis=0)
            part = jnp.dot(
                coup, mapped[u * TB : (u + 1) * TB], preferred_element_type=jnp.float32
            )
            part = jnp.concatenate(
                [
                    part[t * TB : (t + 1) * TB]
                    * boys_ref[0, t * lists + u : t * lists + u + 1, :]
                    for t in range(lists)
                ],
                axis=0,
            )
            total = part if total is None else total + part
        tile = jnp.dot(
            total.astype(jnp.bfloat16), weighted_ref[0], preferred_element_type=jnp.float32
        )
        for c in range(lists):
            for r in range(lists):
                acc[at[c], at[r]] += tile[c * TB : (c + 1) * TB, r * TB : (r + 1) * TB]

    @pl.when(n == pl.num_programs(0) - 1)
    def _():
        def put(index, carry):
            c = index // CL
            r = index % CL
            coded, scale = encode(acc[c, r].T)
            out_ref[c // per, c % per, r] = coded
            scale_ref[c // per, c % per, pl.ds(r, 1), :] = scale
            return carry

        lax.fori_loop(0, CL * CL, put, 0)


def region_exchange(places, count, values, weighted, boys, dens, coup, grid_size):
    batches, points, listed = values.shape
    per = CL // grid_size
    lists = places.shape[1]
    whole = lambda *shape: pl.BlockSpec(shape, lambda n, *_: (0,) * len(shape))
    return pl.pallas_call(
        functools.partial(batch_kernel, per),
        grid_spec=pltpu.PrefetchScalarGridSpec(
            num_scalar_prefetch=2,
            grid=(batches,),
            in_specs=[
                pl.BlockSpec((1, points, listed), lambda n, *_: (n, 0, 0)),
                pl.BlockSpec((1, points, listed), lambda n, *_: (n, 0, 0)),
                pl.BlockSpec((1, lists * lists, points), lambda n, *_: (n, 0, 0)),
                whole(grid_size, per, CL, TB, TB),
                whole(CL, CL, TB, TB),
            ],
            out_specs=[
                whole(grid_size, per, CL, TB, TB),
                whole(grid_size, per, CL, TB),
            ],
            scratch_shapes=[pltpu.VMEM((CL, CL, TB, TB), jnp.float32)],
        ),
        out_shape=[
            jax.ShapeDtypeStruct((grid_size, per, CL, TB, TB), jnp.int16),
            jax.ShapeDtypeStruct((grid_size, per, CL, TB), jnp.float32),
        ],
        compiler_params=pltpu.CompilerParams(vmem_limit_bytes=48 * 1024 * 1024),
        name="region_exchange",
    )(places, count, values, weighted, boys, dens, coup)


def collect_kernel(
    grid_size,
    basis_size,
    owned,
    turns,
    kq,
    ks,
    takes,
    out,
    zq,
    zs,
    sq,
    ss,
    xq,
    xs,
    hq,
    hs,
    wq,
    ws,
    z_send,
    z_recv,
    x_send,
    x_recv,
    w_send,
    w_recv,
):
    per = CL // grid_size
    members = CL // owned
    per_owner = turns * per
    me_grid = lax.axis_index("grid")
    me_basis = lax.axis_index("basis")
    mine = lax.rem(me_basis, members)

    barrier = pltpu.get_barrier_semaphore()
    for d in range(1, grid_size):
        pl.semaphore_signal(
            barrier,
            inc=1,
            device_id=(lax.rem(me_grid + d, grid_size), me_basis),
            device_id_type=pl.DeviceIdType.MESH,
        )
    for d in range(1, basis_size):
        pl.semaphore_signal(
            barrier,
            inc=1,
            device_id=(me_grid, lax.rem(me_basis + d, basis_size)),
            device_id_type=pl.DeviceIdType.MESH,
        )
    pl.semaphore_wait(barrier, grid_size + basis_size - 2)

    def pair(sources, targets, sends, recvs, device):
        return [
            pltpu.make_async_remote_copy(
                src_ref=sources[which],
                dst_ref=targets[which],
                send_sem=sends.at[which],
                recv_sem=recvs.at[which],
                device_id=device,
                device_id_type=pl.DeviceIdType.MESH,
            )
            for which in range(2)
        ]

    def z_copy(cc, d):
        to = lax.rem(me_grid + d, grid_size)
        return pair(
            (kq.at[to, cc], ks.at[to, cc]),
            (zq.at[d - 1, cc], zs.at[d - 1, cc]),
            z_send.at[d - 1, cc],
            z_recv.at[d - 1, cc],
            (to, me_basis),
        )

    def x_copy(cc, d):
        to = lax.rem(me_basis + d, basis_size)
        its = lax.rem(to, members)
        return pair(
            (sq.at[cc, its], ss.at[cc, its]),
            (xq.at[d - 1, cc], xs.at[d - 1, cc]),
            x_send.at[d - 1, cc],
            x_recv.at[d - 1, cc],
            (me_grid, to),
        )

    def w_place(q):
        at = CL * q + me_grid * per
        return at // per_owner, lax.rem(at, per_owner) // per

    def w_copy(cc, q):
        to, slot = w_place(q)
        return pair(
            (hq.at[q, cc], hs.at[q, cc]),
            (wq.at[slot, cc], ws.at[slot, cc]),
            w_send.at[q, cc],
            w_recv.at[slot, cc],
            (to, me_basis),
        )

    def w_arrival(cc, slot):
        return pair(
            (hq.at[slot, cc], hs.at[slot, cc]),
            (wq.at[slot, cc], ws.at[slot, cc]),
            w_send.at[slot, cc],
            w_recv.at[slot, cc],
            (lax.rem(me_grid + 1, grid_size), me_basis),
        )

    def w_from(slot):
        return lax.rem(me_grid * per_owner + slot * per, CL) // per

    for cc in range(per):
        for d in range(1, grid_size):
            for copy in z_copy(cc, d):
                copy.start()

    for cc in range(per):
        for d in range(1, grid_size):
            for copy in z_copy(cc, d):
                copy.wait_recv()
        for m in range(members):

            def add_up(i, carry):
                r = m * owned + i
                total = decode(kq[me_grid, cc, r], ks[me_grid, cc, pl.ds(r, 1), :])
                for d in range(1, grid_size):
                    total += decode(zq[d - 1, cc, r], zs[d - 1, cc, pl.ds(r, 1), :])
                sq[cc, m, i], ss[cc, m, pl.ds(i, 1), :] = encode(total)
                return carry

            lax.fori_loop(0, owned, add_up, 0)
        for d in range(1, basis_size):
            for copy in x_copy(cc, d):
                copy.start()

    for cc in range(per):
        for d in range(1, basis_size):
            for copy in x_copy(cc, d):
                copy.wait_recv()
        for q in range(turns):

            def place(i, carry):
                total = decode(
                    sq[cc, mine, i], ss[cc, mine, pl.ds(i, 1), :] * takes[0, cc, i, q : q + 1, :]
                )
                for d in range(1, basis_size):
                    total += decode(
                        xq[d - 1, cc, i],
                        xs[d - 1, cc, pl.ds(i, 1), :] * takes[d, cc, i, q : q + 1, :],
                    )
                hq[q, cc, i], hs[q, cc, pl.ds(i, 1), :] = encode(total)
                return carry

            lax.fori_loop(0, owned, place, 0)
            to, slot = w_place(q)

            @pl.when(to != me_grid)
            def _():
                for copy in w_copy(cc, q):
                    copy.start()

            @pl.when(to == me_grid)
            def _():
                wq[slot, cc] = hq[q, cc]
                ws[slot, cc] = hs[q, cc]

    for cc in range(per):
        for slot in range(turns):

            @pl.when(w_from(slot) != me_grid)
            def _():
                for copy in w_arrival(cc, slot):
                    copy.wait_recv()

            for i in range(owned):
                out[i * TB : (i + 1) * TB, (slot * per + cc) * TB : (slot * per + cc + 1) * TB] = (
                    decode(wq[slot, cc, i], ws[slot, cc, i : i + 1, :])
                )

    for cc in range(per):
        for d in range(1, grid_size):
            for copy in z_copy(cc, d):
                copy.wait_send()
        for d in range(1, basis_size):
            for copy in x_copy(cc, d):
                copy.wait_send()
        for q in range(turns):

            @pl.when(w_place(q)[0] != me_grid)
            def _():
                for copy in w_copy(cc, q):
                    copy.wait_send()


def collect(coded, scales, takes, grid_size, basis_size, owned, turns):
    per = CL // grid_size
    members = CL // owned
    vmem = pl.BlockSpec(memory_space=pltpu.VMEM)

    def both(*lead):
        return [
            pltpu.VMEM(lead + (TB, TB), jnp.int16),
            pltpu.VMEM(lead + (TB,), jnp.float32),
        ]

    return pl.pallas_call(
        functools.partial(collect_kernel, grid_size, basis_size, owned, turns),
        out_shape=jax.ShapeDtypeStruct((owned * TB, turns * per * TB), jnp.float32),
        in_specs=[vmem] * 3,
        out_specs=vmem,
        scratch_shapes=both(grid_size - 1, per, CL)
        + both(per, members, owned)
        + both(basis_size - 1, per, owned)
        + both(turns, per, owned)
        + both(turns, per, owned)
        + [
            pltpu.SemaphoreType.DMA((grid_size - 1, per, 2)),
            pltpu.SemaphoreType.DMA((grid_size - 1, per, 2)),
            pltpu.SemaphoreType.DMA((basis_size - 1, per, 2)),
            pltpu.SemaphoreType.DMA((basis_size - 1, per, 2)),
            pltpu.SemaphoreType.DMA((turns, per, 2)),
            pltpu.SemaphoreType.DMA((turns, per, 2)),
        ],
        compiler_params=pltpu.CompilerParams(
            collective_id=0, has_side_effects=True, vmem_limit_bytes=48 * 1024 * 1024
        ),
        name="collect",
    )(coded, scales, takes)


def body(
    basis_values,
    weights,
    points,
    block_lists,
    counts,
    density,
    centers,
    block_centers,
    block_exponents,
):
    basis_size = lax.axis_size("basis")
    grid_size = lax.axis_size("grid")
    me_basis = lax.axis_index("basis")
    me_grid = lax.axis_index("grid")
    block_count = block_exponents.shape[0]
    owned_blocks = block_count // basis_size
    turns = block_count // CL
    per = CL // grid_size
    batches, point_total = weights.shape
    lists = block_lists.shape[1]

    first = first_block_of(block_lists, block_count)
    firsts = lax.all_to_all(
        jnp.broadcast_to(first, (basis_size, 1)), "basis", split_axis=0, concat_axis=0, tiled=True
    )[:, 0]
    my_residues = me_grid * per + jnp.arange(per, dtype=jnp.int32)
    columns = block_with_residue(firsts[:, None], my_residues[None, :], block_count)

    members = block_with_residue(first, jnp.arange(CL, dtype=jnp.int32), block_count)
    slots = (me_basis - members // owned_blocks) % basis_size

    coup = region_coupling(members, centers)
    boys = boys_table(
        points.astype(jnp.float32), block_lists, block_centers, block_exponents
    ).reshape(batches, lists * lists, point_total)
    live_count = counts[0, 0]
    is_live = jnp.arange(batches, dtype=jnp.int32) < live_count
    scaled = jnp.where(is_live[:, None], weights, 0.0) / point_total
    weighted = (basis_values * scaled[:, :, None]).astype(jnp.bfloat16)

    packed = pack_density(columns, density)
    dens = fetch_density(slots, packed, grid_size, basis_size, owned_blocks)
    coded, scales = region_exchange(
        block_lists % CL, counts.reshape(1), basis_values, weighted, boys, dens, coup, grid_size
    )
    back = (me_basis - jnp.arange(basis_size, dtype=jnp.int32)) % basis_size
    begins = firsts[back]
    my_blocks = me_basis * owned_blocks + jnp.arange(owned_blocks, dtype=jnp.int32)
    inside = (my_blocks[None, :] - begins[:, None]) % block_count < CL
    turn_at = block_with_residue(begins[:, None], my_residues[None, :], block_count) // CL
    takes = (
        inside[:, None, :, None]
        & (turn_at[:, :, None, None] == jnp.arange(turns, dtype=jnp.int32)[None, None, None, :])
    )
    takes = jnp.broadcast_to(
        takes.astype(jnp.float32)[..., None], takes.shape + (TB,)
    )
    return collect(coded, scales, takes, grid_size, basis_size, owned_blocks, turns)


def solution(mesh):
    placed = (
        P(("grid", "basis"), None, None),
        P(("grid", "basis"), None),
        P(("grid", "basis"), None, None),
        P(("grid", "basis"), None),
        P("basis", "grid"),
        P("basis", None),
        P(),
        P(),
        P(),
    )
    return jax.shard_map(
        body, mesh=mesh, in_specs=placed, out_specs=P("basis", "grid"), check_vma=False
    )
```

profile of v0, /device:TPU:27, one launch (start us, length us, event | category | flops | bytes accessed | tf_op | source)
XLA Modules:
  0.0 190.5 jit_solution(18254314505405961313)
XLA Ops:
  0.0 0.0 copy-start
  0.0 0.8 copy.67
  0.8 0.1 eq.47
  0.9 0.1 fusion.2
  1.0 0.6 slice.8
  1.6 1.4 fusion.22
  3.0 1.3 broadcast_in_dim.26
  4.3 4.5 %all-to-all-start = ((s32[8,1,1]{2,1,0:T(1,128)}), s32[8,1,1]{2,1,0:T(1,128)S(1)}, u32[]{:S(2)}, u32[]{:S(2)}) async-start(s32[8,1,1]{2,1,0:T(1,128)} %broadcast_in_dim.26), calls=%async_computation | async-start | bytes 8192 | tf_op jit(solution)/shard_map/all_to_all | solution.py:562
  8.8 0.7 and_select_fusion.1
  9.6 0.1 iota_add_fusion
  9.7 1.5 copy.80
  11.2 2.8 %gather_fusion.2 = f32[1024,3]{1,0:T(8,128)S(1)} fusion(f32[3,4096]{0,1:T(8,128)S(1)} %copy.80, s32[1024]{0:T(1024)S(1)} %broadcast_clamp_fusion), kind=kCustom, calls=%fused_computation.2 | custom fusion | bytes 28672 | tf_op jit(solution)/shard_map/gather | solution.py:42
  14.0 0.2 copy.81
  14.2 1.3 multiply_reduce_fusion
  15.4 0.0 copy-start.4
  15.5 0.0 copy-start.2
  15.5 1.9 %exponential_convert_fusion.coup_ref = bf16[8,8,128,128]{3,2,1,0:T(8,128)(2,1)} fusion(f32[8,8,128,128]{3,2,1,0:T(8,128)S(1)} %multiply_reduce_fusion), kind=kLoop, calls=%fused_computation.6 | loop fusion | flops 2097152 | bytes 6291456 | tf_op jit(solution)/shard_map/convert_element_type | solution.py:46
  17.4 0.1 reshape.276
  17.5 0.0 copy-done.4
  17.5 0.1 copy.75
  17.6 0.6 gather_fusion.1
  18.2 0.1 copy.76
  18.3 0.0 copy-done.2
  18.3 0.0 copy-done
  18.3 0.0 copy-start.3
  18.4 0.8 gather_fusion
  19.1 0.1 reshape.275
  19.2 0.1 copy.72
  19.3 0.1 copy.74
  20.1 0.2 multiply_reduce_fusion.1
  20.3 0.2 multiply_divide_fusion.boys_ref
  20.5 0.0 copy-done.3
  20.5 0.1 select_multiply_fusion
  20.6 4.0 %multiply_convert_fusion.weighted_ref = bf16[16,256,512]{2,1,0:T(8,128)(2,1)} fusion(bf16[16,256,512]{2,1,0:T(8,128)(2,1)} %values_ref.1, f32[16,256]{1,0:T(8,128)S(1)} %select_multiply_fusion), kind=kLoop, calls=%fused_computation.5 | loop fusion | flops 6291456 | bytes 8404992 | tf_op jit(solution)/shard_map/convert_element_type | solution.py:578
  24.6 0.0 all-to-all-done
  24.6 0.2 reduce
  24.8 0.7 gather_fusion.3
  25.5 0.7 add_select_fusion.1
  26.2 0.1 iota_compare_fusion.1
  26.2 0.1 fusion.6
  26.3 3.8 %pack_density.1.packed = bf16[8,2,512,128]{3,2,1,0:T(8,128)(2,1)} custom-call(s32[8,2]{1,0:T(8,128)} %get-tuple-element.12.column_ref, bf16[512,4096]{1,0:T(8,128)(2,1)} %dens_ref.1), custom_call_target="tpu_custom_call" | custom-call | tf_op jit(solution)/shard_map/pack_density/pallas_call | solution.py:69
  30.2 0.0 copy-start.1
  30.2 1.6 copy-done.1
  31.8 52.0 %fetch_density.1.dens_ref = bf16[4,2,8,128,128]{4,3,2,1,0:T(8,128)(2,1)S(1)} custom-call(s32[8]{0:T(128)S(1)} %get-tuple-element.13.slot_ref, bf16[8,2,512,128]{3,2,1,0:T(8,128)(2,1)S(1)} %copy-done.1), custom_call_target="tpu_custom_call" | custom-call | tf_op jit(solution)/shard_map/fetch_density/pallas_call | solution.py:191
  83.8 0.1 and_convert_fusion
  83.8 21.7 %region_exchange.1 = (s16[4,2,8,128,128]{4,3,2,1,0:T(8,128)(2,1)S(1)}, f32[4,2,8,128]{3,2,1,0:T(8,128)S(1)}) custom-call(s32[16,4]{1,0:T(8,128)S(1)} %get-tuple-element.10.place_ref, s32[1]{0:T(128)} %bitcast.17.count_ref, bf16[16,256,512]{2,1,0:T(8,128)(2,1)} %values_ref.1, bf16[16,256,512]{2,1,0:T(8,128)(2,1)} %multiply_convert_fusion.weighted_ref, ...), custom_call_target="tpu_custom_call" | custom-call | tf_op jit(solution)/shard_map/region_exchange/pallas_call | solution.py:283
  105.5 0.1 broadcast_in_dim.27.takes
  105.7 83.5 %collect.1 = f32[512,1024]{1,0:T(8,128)S(1)} custom-call(s16[4,2,8,128,128]{4,3,2,1,0:T(8,128)(2,1)S(1)} %get-tuple-element.7.kq, f32[4,2,8,128]{3,2,1,0:T(8,128)S(1)} %get-tuple-element.8.ks, f32[8,2,4,4,128]{4,3,2,1,0:T(4,128)S(1)} %broadcast_in_dim.27.takes), custom_call_target="tpu_custom_call" | custom-call | tf_op jit(solution)/shard_map/collect/pallas_call | solution.py:514
  189.2 1.3 copy.93
  (12 shorter events, 0.1 us)
Async XLA Ops:
  0.0 18.3 %copy-start = (f32[32]{0:T(128)S(1)}, f32[32]{0:T(128)}, u32[]{:S(2)}) copy-start(f32[32]{0:T(128)} %param.17) | copy-start | bytes 388
  4.3 20.3 %all-to-all-start = ((s32[8,1,1]{2,1,0:T(1,128)}), s32[8,1,1]{2,1,0:T(1,128)S(1)}, u32[]{:S(2)}, u32[]{:S(2)}) async-start(s32[8,1,1]{2,1,0:T(1,128)} %broadcast_in_dim.26), calls=%async_computation | async-start | bytes 8192 | tf_op jit(solution)/shard_map/all_to_all | solution.py:562
  15.4 2.1 %copy-start.4 = (f32[3,32]{1,0:T(4,128)S(1)}, f32[3,32]{1,0:T(4,128)}, u32[]{:S(2)}) copy-start(f32[3,32]{1,0:T(4,128)} %param.16) | copy-start | bytes 1156
  15.5 2.9 %copy-start.2 = (bf16[16,3,256]{2,0,1:T(8,128)(2,1)S(1)}, bf16[16,3,256]{2,0,1:T(8,128)(2,1)}, u32[]{:S(2)}) copy-start(bf16[16,3,256]{2,0,1:T(8,128)(2,1)} %param.11) | copy-start | bytes 73732
  18.3 2.2 %copy-start.3 = (f32[16,256]{1,0:T(8,128)S(1)}, f32[16,256]{1,0:T(8,128)}, u32[]{:S(2)}) copy-start(f32[16,256]{1,0:T(8,128)} %param.10) | copy-start | bytes 49156
  30.2 1.6 copy-start.1
where the time goes:
time: 191 us
  Pallas kernels  161 us (84%)
  local copies, waits for them, and re-layouts  12.8 us (7%)
  other arithmetic  11.3 us (6%)
  starting transfers between devices  4.53 us (2%)
    pallas_call x1, Pallas kernels, collect(): pl.pallas_call(functools.partial(collect_kernel, grid_size, basis_size, o...  83.5 us
    pallas_call x1, Pallas kernels, fetch_density(): pl.pallas_call(functools.partial(fetch_kernel, grid_size, basis_size, own...  52 us
    pallas_call x1, Pallas kernels, region_exchange(): pl.pallas_call(functools.partial(batch_kernel, per), grid_spec=pltpu.Pref...  21.7 us
    unnamed x14, local copies, waits for them, and re-layouts  5.26 us
    all_to_all x1, starting transfers between devices, body(): lax.all_to_all(jnp.broadcast_to(first, (basis_size, 1)), 'basis', split_a...  4.53 us
    convert_element_type x1, other arithmetic, body(): weighted = (basis_values * scaled[:, :, None]).astype(jnp.bfloat16)  4 us
    pallas_call x1, Pallas kernels, pack_density(): pl.pallas_call(pack_kernel, in_specs=[pl.BlockSpec(memory_space=pltpu.SME...  3.85 us
  transfers between devices with their start and end apart: 1, of which 0 were waited for; matrix products, arithmetic and copies ran while one was open for 8% of the time, Pallas kernels for 0%

commit v1 on v0

--- a/solution.py
+++ b/solution.py
@@ -222,14 +222,14 @@
 ):
     n = pl.program_id(0)
     lists = place_ref.shape[1]
+    group = values_ref.shape[0]
 
     @pl.when(n == 0)
     def _():
         acc[...] = jnp.zeros_like(acc)
 
-    @pl.when(n < count_ref[0])
-    def _():
-        at = [place_ref[n, t] for t in range(lists)]
+    def one(b):
+        at = [place_ref[n * group + b, t] for t in range(lists)]
         dens = jnp.concatenate(
             [
                 jnp.concatenate([dens_ref[c // per, c % per, r] for c in at], axis=1)
@@ -238,7 +238,7 @@
             axis=0,
         )
         mapped = lax.dot_general(
-            dens, values_ref[0], (((1,), (1,)), ((), ())), preferred_element_type=jnp.float32
+            dens, values_ref[b], (((1,), (1,)), ((), ())), preferred_element_type=jnp.float32
         ).astype(jnp.bfloat16)
         total = None
         for u in range(lists):
@@ -249,18 +249,23 @@
             part = jnp.concatenate(
                 [
                     part[t * TB : (t + 1) * TB]
-                    * boys_ref[0, t * lists + u : t * lists + u + 1, :]
+                    * boys_ref[b, t * lists + u : t * lists + u + 1, :]
                     for t in range(lists)
                 ],
                 axis=0,
             )
             total = part if total is None else total + part
         tile = jnp.dot(
-            total.astype(jnp.bfloat16), weighted_ref[0], preferred_element_type=jnp.float32
-        )
-        for c in range(lists):
-            for r in range(lists):
-                acc[at[c], at[r]] += tile[c * TB : (c + 1) * TB, r * TB : (r + 1) * TB]
+            total.astype(jnp.bfloat16), weighted_ref[b], preferred_element_type=jnp.float32
+        )
+        return at, tile
+
+    @pl.when(n * group < count_ref[0])
+    def _():
+        for at, tile in [one(b) for b in range(group)]:
+            for c in range(lists):
+                for r in range(lists):
+                    acc[at[c], at[r]] += tile[c * TB : (c + 1) * TB, r * TB : (r + 1) * TB]
 
     @pl.when(n == pl.num_programs(0) - 1)
     def _():
@@ -279,16 +284,17 @@
     batches, points, listed = values.shape
     per = CL // grid_size
     lists = places.shape[1]
+    group = math.gcd(batches, 2)
     whole = lambda *shape: pl.BlockSpec(shape, lambda n, *_: (0,) * len(shape))
     return pl.pallas_call(
         functools.partial(batch_kernel, per),
         grid_spec=pltpu.PrefetchScalarGridSpec(
             num_scalar_prefetch=2,
-            grid=(batches,),
+            grid=(batches // group,),
             in_specs=[
-                pl.BlockSpec((1, points, listed), lambda n, *_: (n, 0, 0)),
-                pl.BlockSpec((1, points, listed), lambda n, *_: (n, 0, 0)),
-                pl.BlockSpec((1, lists * lists, points), lambda n, *_: (n, 0, 0)),
+                pl.BlockSpec((group, points, listed), lambda n, *_: (n, 0, 0)),
+                pl.BlockSpec((group, points, listed), lambda n, *_: (n, 0, 0)),
+                pl.BlockSpec((group, lists * lists, points), lambda n, *_: (n, 0, 0)),
                 whole(grid_size, per, CL, TB, TB),
                 whole(CL, CL, TB, TB),
             ],
@@ -318,6 +324,8 @@
     out,
     zq,
     zs,
+    yq,
+    ys,
     sq,
     ss,
     xq,
@@ -370,15 +378,37 @@
             for which in range(2)
         ]
 
-    def z_copy(cc, d):
-        to = lax.rem(me_grid + d, grid_size)
+    def z_copy(cc, j, side, fresh):
+        to = lax.rem(me_grid + (1 if side == 0 else grid_size - 1), grid_size)
         return pair(
-            (kq.at[to, cc], ks.at[to, cc]),
-            (zq.at[d - 1, cc], zs.at[d - 1, cc]),
-            z_send.at[d - 1, cc],
-            z_recv.at[d - 1, cc],
+            (kq.at[j, cc], ks.at[j, cc]) if fresh else (yq.at[side, j, cc], ys.at[side, j, cc]),
+            (zq.at[side, j, cc], zs.at[side, j, cc]),
+            z_send.at[side, j, cc],
+            z_recv.at[side, j, cc],
             (to, me_basis),
         )
+
+    last = grid_size - 1
+
+    def pass_on(cc, j, side):
+        more = (me_grid > 0) & (me_grid < j) if side == 0 else (me_grid < last) & (me_grid > j)
+
+        @pl.when(more)
+        def _():
+            for copy in z_copy(cc, j, side, False):
+                copy.wait_recv()
+
+            def add_own(r, carry):
+                row = pl.ds(r, 1)
+                yq[side, j, cc, r], ys[side, j, cc, row, :] = encode(
+                    decode(kq[j, cc, r], ks[j, cc, row, :])
+                    + decode(zq[side, j, cc, r], zs[side, j, cc, row, :])
+                )
+                return carry
+
+            lax.fori_loop(0, CL, add_own, 0)
+            for copy in z_copy(cc, j, side, False):
+                copy.start()
 
     def x_copy(cc, d):
         to = lax.rem(me_basis + d, basis_size)
@@ -417,22 +447,48 @@
     def w_from(slot):
         return lax.rem(me_grid * per_owner + slot * per, CL) // per
 
+    @pl.when(me_grid == 0)
+    def _():
+        for cc in range(per):
+            for j in range(last, 0, -1):
+                for copy in z_copy(cc, j, 0, True):
+                    copy.start()
+        zq[0, 0] = jnp.zeros(zq.shape[2:], zq.dtype)
+        zs[0, 0] = jnp.zeros(zs.shape[2:], zs.dtype)
+
+    @pl.when(me_grid == last)
+    def _():
+        for cc in range(per):
+            for j in range(last):
+                for copy in z_copy(cc, j, 1, True):
+                    copy.start()
+        zq[1, last] = jnp.zeros(zq.shape[2:], zq.dtype)
+        zs[1, last] = jnp.zeros(zs.shape[2:], zs.dtype)
+
     for cc in range(per):
-        for d in range(1, grid_size):
-            for copy in z_copy(cc, d):
-                copy.start()
-
-    for cc in range(per):
-        for d in range(1, grid_size):
-            for copy in z_copy(cc, d):
+        for k in range(last):
+            pass_on(cc, last - k, 0)
+            pass_on(cc, k, 1)
+
+        @pl.when(me_grid > 0)
+        def _():
+            for copy in z_copy(cc, me_grid, 0, False):
                 copy.wait_recv()
+
+        @pl.when(me_grid < last)
+        def _():
+            for copy in z_copy(cc, me_grid, 1, False):
+                copy.wait_recv()
+
         for m in range(members):
 
             def add_up(i, carry):
                 r = m * owned + i
                 total = decode(kq[me_grid, cc, r], ks[me_grid, cc, pl.ds(r, 1), :])
-                for d in range(1, grid_size):
-                    total += decode(zq[d - 1, cc, r], zs[d - 1, cc, pl.ds(r, 1), :])
+                for side in range(2):
+                    total += decode(
+                        zq[side, me_grid, cc, r], zs[side, me_grid, cc, pl.ds(r, 1), :]
+                    )
                 sq[cc, m, i], ss[cc, m, pl.ds(i, 1), :] = encode(total)
                 return carry
 
@@ -486,9 +542,18 @@
                 )
 
     for cc in range(per):
-        for d in range(1, grid_size):
-            for copy in z_copy(cc, d):
-                copy.wait_send()
+        for j in range(grid_size):
+
+            @pl.when(me_grid < j)
+            def _():
+                for copy in z_copy(cc, j, 0, False):
+                    copy.wait_send()
+
+            @pl.when(me_grid > j)
+            def _():
+                for copy in z_copy(cc, j, 1, False):
+                    copy.wait_send()
+
         for d in range(1, basis_size):
             for copy in x_copy(cc, d):
                 copy.wait_send()
@@ -516,14 +581,15 @@
         out_shape=jax.ShapeDtypeStruct((owned * TB, turns * per * TB), jnp.float32),
         in_specs=[vmem] * 3,
         out_specs=vmem,
-        scratch_shapes=both(grid_size - 1, per, CL)
+        scratch_shapes=both(2, grid_size, per, CL)
+        + both(2, grid_size, per, CL)
         + both(per, members, owned)
         + both(basis_size - 1, per, owned)
         + both(turns, per, owned)
         + both(turns, per, owned)
         + [
-            pltpu.SemaphoreType.DMA((grid_size - 1, per, 2)),
-            pltpu.SemaphoreType.DMA((grid_size - 1, per, 2)),
+            pltpu.SemaphoreType.DMA((2, grid_size, per, 2)),
+            pltpu.SemaphoreType.DMA((2, grid_size, per, 2)),
             pltpu.SemaphoreType.DMA((basis_size - 1, per, 2)),
             pltpu.SemaphoreType.DMA((basis_size - 1, per, 2)),
             pltpu.SemaphoreType.DMA((turns, per, 2)),

time: 191 us -> 200 us (1.047)
  Pallas kernels: 161 us -> 168 us
    pallas_call x1, Pallas kernels: 83.5 us -> 93.7 us  [collect(): pl.pallas_call(functools.partial(collect_kernel, grid_size, basis_size, o...]
    pallas_call x1, Pallas kernels: 21.7 us -> 18.7 us  [region_exchange(): pl.pallas_call(functools.partial(batch_kernel, per), grid_spec=pltpu.Pref...]
where the time goes in v1:
time: 200 us; the launch traced here: 198 us
  Pallas kernels  168 us (84%)
  local copies, waits for them, and re-layouts  12.8 us (6%)
  other arithmetic  11.3 us (6%)
  starting transfers between devices  4.53 us (2%)
    pallas_call x1, Pallas kernels, collect(): pl.pallas_call(functools.partial(collect_kernel, grid_size, basis_size, o...  93.7 us
    pallas_call x1, Pallas kernels, fetch_density(): pl.pallas_call(functools.partial(fetch_kernel, grid_size, basis_size, own...  52 us
    pallas_call x1, Pallas kernels, region_exchange(): pl.pallas_call(functools.partial(batch_kernel, per), grid_spec=pltpu.Pref...  18.7 us
    unnamed x14, local copies, waits for them, and re-layouts  5.26 us
    all_to_all x1, starting transfers between devices, body(): lax.all_to_all(jnp.broadcast_to(first, (basis_size, 1)), 'basis', split_a...  4.53 us
    convert_element_type x1, other arithmetic, body(): weighted = (basis_values * scaled[:, :, None]).astype(jnp.bfloat16)  4 us
  transfers between devices with their start and end apart: 1, of which 0 were waited for; matrix products, arithmetic and copies ran while one was open for 8% of the time, Pallas kernels for 0%

profile of v1, /device:TPU:27, one launch (start us, length us, event | category | flops | bytes accessed | tf_op | source)
XLA Modules:
  0.0 197.7 jit_solution(4257634341440618315)
XLA Ops:
  0.0 0.0 copy-start
  0.0 0.8 copy.67
  0.8 0.1 eq.47
  0.9 0.1 fusion.2
  1.0 0.6 slice.8
  1.6 1.4 fusion.22
  3.0 1.3 broadcast_in_dim.26
  4.3 4.5 %all-to-all-start = ((s32[8,1,1]{2,1,0:T(1,128)}), s32[8,1,1]{2,1,0:T(1,128)S(1)}, u32[]{:S(2)}, u32[]{:S(2)}) async-start(s32[8,1,1]{2,1,0:T(1,128)} %broadcast_in_dim.26), calls=%async_computation | async-start | bytes 8192 | tf_op jit(solution)/shard_map/all_to_all | solution.py:628
  8.8 0.7 and_select_fusion.1
  9.6 0.1 iota_add_fusion
  9.7 1.5 copy.80
  11.2 2.8 %gather_fusion.2 = f32[1024,3]{1,0:T(8,128)S(1)} fusion(f32[3,4096]{0,1:T(8,128)S(1)} %copy.80, s32[1024]{0:T(1024)S(1)} %broadcast_clamp_fusion), kind=kCustom, calls=%fused_computation.2 | custom fusion | bytes 28672 | tf_op jit(solution)/shard_map/gather | solution.py:42
  14.0 0.2 copy.81
  14.2 1.3 multiply_reduce_fusion
  15.4 0.0 copy-start.4
  15.5 0.0 copy-start.2
  15.5 1.9 exponential_convert_fusion.coup_ref
  17.4 0.1 reshape.276
  17.5 0.0 copy-done.4
  17.5 0.1 copy.75
  17.6 0.6 gather_fusion.1
  18.2 0.1 copy.76
  18.3 0.0 copy-done.2
  18.3 0.0 copy-done
  18.3 0.0 copy-start.3
  18.4 0.8 gather_fusion
  19.1 0.1 reshape.275
  19.2 0.1 copy.72
  19.3 0.1 copy.74
  20.1 0.2 multiply_reduce_fusion.1
  20.3 0.2 multiply_divide_fusion.boys_ref
  20.5 0.0 copy-done.3
  20.5 0.1 select_multiply_fusion
  20.6 4.0 %multiply_convert_fusion.weighted_ref = bf16[16,256,512]{2,1,0:T(8,128)(2,1)} fusion(bf16[16,256,512]{2,1,0:T(8,128)(2,1)} %values_ref.1, f32[16,256]{1,0:T(8,128)S(1)} %select_multiply_fusion), kind=kLoop, calls=%fused_computation.5 | loop fusion | flops 6291456 | bytes 8404992 | tf_op jit(solution)/shard_map/convert_element_type | solution.py:644
  24.6 0.0 all-to-all-done
  24.6 0.2 reduce
  24.8 0.7 gather_fusion.3
  25.5 0.7 add_select_fusion.1
  26.2 0.1 iota_compare_fusion.1
  26.3 0.1 fusion.6
  26.3 3.8 %pack_density.1.packed = bf16[8,2,512,128]{3,2,1,0:T(8,128)(2,1)} custom-call(s32[8,2]{1,0:T(8,128)} %get-tuple-element.12.column_ref, bf16[512,4096]{1,0:T(8,128)(2,1)} %dens_ref.1), custom_call_target="tpu_custom_call" | custom-call | tf_op jit(solution)/shard_map/pack_density/pallas_call | solution.py:69
  30.2 0.0 copy-start.1
  30.2 1.6 copy-done.1
  31.8 52.0 %fetch_density.1.dens_ref = bf16[4,2,8,128,128]{4,3,2,1,0:T(8,128)(2,1)S(1)} custom-call(s32[8]{0:T(128)S(1)} %get-tuple-element.13.slot_ref, bf16[8,2,512,128]{3,2,1,0:T(8,128)(2,1)S(1)} %copy-done.1), custom_call_target="tpu_custom_call" | custom-call | tf_op jit(solution)/shard_map/fetch_density/pallas_call | solution.py:191
  83.8 0.1 and_convert_fusion
  83.8 18.7 %region_exchange.1 = (s16[4,2,8,128,128]{4,3,2,1,0:T(8,128)(2,1)S(1)}, f32[4,2,8,128]{3,2,1,0:T(8,128)S(1)}) custom-call(s32[16,4]{1,0:T(8,128)S(1)} %get-tuple-element.10.place_ref, s32[1]{0:T(128)} %bitcast.17.count_ref, bf16[16,256,512]{2,1,0:T(8,128)(2,1)} %values_ref.1, bf16[16,256,512]{2,1,0:T(8,128)(2,1)} %multiply_convert_fusion.weighted_ref, ...), custom_call_target="tpu_custom_call" | custom-call | tf_op jit(solution)/shard_map/region_exchange/pallas_call | solution.py:289
  102.5 0.1 broadcast_in_dim.27.takes
  102.7 93.7 %collect.1 = f32[512,1024]{1,0:T(8,128)S(1)} custom-call(s16[4,2,8,128,128]{4,3,2,1,0:T(8,128)(2,1)S(1)} %get-tuple-element.7.kq, f32[4,2,8,128]{3,2,1,0:T(8,128)S(1)} %get-tuple-element.8.ks, f32[8,2,4,4,128]{4,3,2,1,0:T(4,128)S(1)} %broadcast_in_dim.27.takes), custom_call_target="tpu_custom_call" | custom-call | tf_op jit(solution)/shard_map/collect/pallas_call | solution.py:579
  196.3 1.3 copy.93
  (12 shorter events, 0.1 us)
Async XLA Ops:
  0.0 18.3 %copy-start = (f32[32]{0:T(128)S(1)}, f32[32]{0:T(128)}, u32[]{:S(2)}) copy-start(f32[32]{0:T(128)} %param.17) | copy-start | bytes 388
  4.3 20.3 %all-to-all-start = ((s32[8,1,1]{2,1,0:T(1,128)}), s32[8,1,1]{2,1,0:T(1,128)S(1)}, u32[]{:S(2)}, u32[]{:S(2)}) async-start(s32[8,1,1]{2,1,0:T(1,128)} %broadcast_in_dim.26), calls=%async_computation | async-start | bytes 8192 | tf_op jit(solution)/shard_map/all_to_all | solution.py:628
  15.4 2.1 %copy-start.4 = (f32[3,32]{1,0:T(4,128)S(1)}, f32[3,32]{1,0:T(4,128)}, u32[]{:S(2)}) copy-start(f32[3,32]{1,0:T(4,128)} %param.16) | copy-start | bytes 1156
  15.5 2.9 %copy-start.2 = (bf16[16,3,256]{2,0,1:T(8,128)(2,1)S(1)}, bf16[16,3,256]{2,0,1:T(8,128)(2,1)}, u32[]{:S(2)}) copy-start(bf16[16,3,256]{2,0,1:T(8,128)(2,1)} %param.11) | copy-start | bytes 73732
  18.3 2.2 %copy-start.3 = (f32[16,256]{1,0:T(8,128)S(1)}, f32[16,256]{1,0:T(8,128)}, u32[]{:S(2)}) copy-start(f32[16,256]{1,0:T(8,128)} %param.10) | copy-start | bytes 49156
  30.2 1.6 copy-start.1

commit v2 on v0

--- a/solution.py
+++ b/solution.py
@@ -218,18 +218,20 @@
 
 
 def batch_kernel(
-    per, place_ref, count_ref, values_ref, weighted_ref, boys_ref, dens_ref, coup_ref, out_ref, scale_ref, acc
+    per, owned, place_ref, count_ref, values_ref, weighted_ref, boys_ref, dens_ref, coup_ref, out_ref, scale_ref, acc
 ):
     n = pl.program_id(0)
     lists = place_ref.shape[1]
+    group = values_ref.shape[0]
+    halves = math.gcd(owned, 2)
+    width = owned // halves
 
     @pl.when(n == 0)
     def _():
         acc[...] = jnp.zeros_like(acc)
 
-    @pl.when(n < count_ref[0])
-    def _():
-        at = [place_ref[n, t] for t in range(lists)]
+    def one(b):
+        at = [place_ref[n * group + b, t] for t in range(lists)]
         dens = jnp.concatenate(
             [
                 jnp.concatenate([dens_ref[c // per, c % per, r] for c in at], axis=1)
@@ -238,7 +240,7 @@
             axis=0,
         )
         mapped = lax.dot_general(
-            dens, values_ref[0], (((1,), (1,)), ((), ())), preferred_element_type=jnp.float32
+            dens, values_ref[b], (((1,), (1,)), ((), ())), preferred_element_type=jnp.float32
         ).astype(jnp.bfloat16)
         total = None
         for u in range(lists):
@@ -249,18 +251,23 @@
             part = jnp.concatenate(
                 [
                     part[t * TB : (t + 1) * TB]
-                    * boys_ref[0, t * lists + u : t * lists + u + 1, :]
+                    * boys_ref[b, t * lists + u : t * lists + u + 1, :]
                     for t in range(lists)
                 ],
                 axis=0,
             )
             total = part if total is None else total + part
         tile = jnp.dot(
-            total.astype(jnp.bfloat16), weighted_ref[0], preferred_element_type=jnp.float32
-        )
-        for c in range(lists):
-            for r in range(lists):
-                acc[at[c], at[r]] += tile[c * TB : (c + 1) * TB, r * TB : (r + 1) * TB]
+            total.astype(jnp.bfloat16), weighted_ref[b], preferred_element_type=jnp.float32
+        )
+        return at, tile
+
+    @pl.when(n * group < count_ref[0])
+    def _():
+        for at, tile in [one(b) for b in range(group)]:
+            for c in range(lists):
+                for r in range(lists):
+                    acc[at[c], at[r]] += tile[c * TB : (c + 1) * TB, r * TB : (r + 1) * TB]
 
     @pl.when(n == pl.num_programs(0) - 1)
     def _():
@@ -268,39 +275,45 @@
             c = index // CL
             r = index % CL
             coded, scale = encode(acc[c, r].T)
-            out_ref[c // per, c % per, r] = coded
-            scale_ref[c // per, c % per, pl.ds(r, 1), :] = scale
+            part = r % owned // width
+            unit = c % per * halves + part
+            row = r // owned * width + r % width
+            out_ref[c // per, unit, row] = coded
+            scale_ref[c // per, unit, pl.ds(row, 1), :] = scale
             return carry
 
         lax.fori_loop(0, CL * CL, put, 0)
 
 
-def region_exchange(places, count, values, weighted, boys, dens, coup, grid_size):
+def region_exchange(places, count, values, weighted, boys, dens, coup, grid_size, owned):
     batches, points, listed = values.shape
     per = CL // grid_size
     lists = places.shape[1]
+    group = math.gcd(batches, 2)
+    halves = math.gcd(owned, 2)
+    units, rows = per * halves, CL // halves
     whole = lambda *shape: pl.BlockSpec(shape, lambda n, *_: (0,) * len(shape))
     return pl.pallas_call(
-        functools.partial(batch_kernel, per),
+        functools.partial(batch_kernel, per, owned),
         grid_spec=pltpu.PrefetchScalarGridSpec(
             num_scalar_prefetch=2,
-            grid=(batches,),
+            grid=(batches // group,),
             in_specs=[
-                pl.BlockSpec((1, points, listed), lambda n, *_: (n, 0, 0)),
-                pl.BlockSpec((1, points, listed), lambda n, *_: (n, 0, 0)),
-                pl.BlockSpec((1, lists * lists, points), lambda n, *_: (n, 0, 0)),
+                pl.BlockSpec((group, points, listed), lambda n, *_: (n, 0, 0)),
+                pl.BlockSpec((group, points, listed), lambda n, *_: (n, 0, 0)),
+                pl.BlockSpec((group, lists * lists, points), lambda n, *_: (n, 0, 0)),
                 whole(grid_size, per, CL, TB, TB),
                 whole(CL, CL, TB, TB),
             ],
             out_specs=[
-                whole(grid_size, per, CL, TB, TB),
-                whole(grid_size, per, CL, TB),
+                whole(grid_size, units, rows, TB, TB),
+                whole(grid_size, units, rows, TB),
             ],
             scratch_shapes=[pltpu.VMEM((CL, CL, TB, TB), jnp.float32)],
         ),
         out_shape=[
-            jax.ShapeDtypeStruct((grid_size, per, CL, TB, TB), jnp.int16),
-            jax.ShapeDtypeStruct((grid_size, per, CL, TB), jnp.float32),
+            jax.ShapeDtypeStruct((grid_size, units, rows, TB, TB), jnp.int16),
+            jax.ShapeDtypeStruct((grid_size, units, rows, TB), jnp.float32),
         ],
         compiler_params=pltpu.CompilerParams(vmem_limit_bytes=48 * 1024 * 1024),
         name="region_exchange",
@@ -336,6 +349,9 @@
     per = CL // grid_size
     members = CL // owned
     per_owner = turns * per
+    halves = math.gcd(owned, 2)
+    width = owned // halves
+    units = per * halves
     me_grid = lax.axis_index("grid")
     me_basis = lax.axis_index("basis")
     mine = lax.rem(me_basis, members)
@@ -417,31 +433,31 @@
     def w_from(slot):
         return lax.rem(me_grid * per_owner + slot * per, CL) // per
 
-    for cc in range(per):
+    for cc in range(units):
         for d in range(1, grid_size):
             for copy in z_copy(cc, d):
                 copy.start()
 
-    for cc in range(per):
+    for cc in range(units):
         for d in range(1, grid_size):
             for copy in z_copy(cc, d):
                 copy.wait_recv()
         for m in range(members):
 
             def add_up(i, carry):
-                r = m * owned + i
+                r = m * width + i
                 total = decode(kq[me_grid, cc, r], ks[me_grid, cc, pl.ds(r, 1), :])
                 for d in range(1, grid_size):
                     total += decode(zq[d - 1, cc, r], zs[d - 1, cc, pl.ds(r, 1), :])
                 sq[cc, m, i], ss[cc, m, pl.ds(i, 1), :] = encode(total)
                 return carry
 
-            lax.fori_loop(0, owned, add_up, 0)
+            lax.fori_loop(0, width, add_up, 0)
         for d in range(1, basis_size):
             for copy in x_copy(cc, d):
                 copy.start()
 
-    for cc in range(per):
+    for cc in range(units):
         for d in range(1, basis_size):
             for copy in x_copy(cc, d):
                 copy.wait_recv()
@@ -449,17 +465,17 @@
 
             def place(i, carry):
                 total = decode(
-                    sq[cc, mine, i], ss[cc, mine, pl.ds(i, 1), :] * takes[0, cc, i, q : q + 1, :]
+                    sq[cc, mine, i], ss[cc, mine, pl.ds(i, 1), :] * takes[0, cc // halves, cc % halves * width + i, q : q + 1, :]
                 )
                 for d in range(1, basis_size):
                     total += decode(
                         xq[d - 1, cc, i],
-                        xs[d - 1, cc, pl.ds(i, 1), :] * takes[d, cc, i, q : q + 1, :],
+                        xs[d - 1, cc, pl.ds(i, 1), :] * takes[d, cc // halves, cc % halves * width + i, q : q + 1, :],
                     )
                 hq[q, cc, i], hs[q, cc, pl.ds(i, 1), :] = encode(total)
                 return carry
 
-            lax.fori_loop(0, owned, place, 0)
+            lax.fori_loop(0, width, place, 0)
             to, slot = w_place(q)
 
             @pl.when(to != me_grid)
@@ -472,7 +488,7 @@
                 wq[slot, cc] = hq[q, cc]
                 ws[slot, cc] = hs[q, cc]
 
-    for cc in range(per):
+    for cc in range(units):
         for slot in range(turns):
 
             @pl.when(w_from(slot) != me_grid)
@@ -480,12 +496,14 @@
                 for copy in w_arrival(cc, slot):
                     copy.wait_recv()
 
-            for i in range(owned):
-                out[i * TB : (i + 1) * TB, (slot * per + cc) * TB : (slot * per + cc + 1) * TB] = (
-                    decode(wq[slot, cc, i], ws[slot, cc, i : i + 1, :])
+            column = (slot * per + cc // halves) * TB
+            for i in range(width):
+                row = (cc % halves * width + i) * TB
+                out[row : row + TB, column : column + TB] = decode(
+                    wq[slot, cc, i], ws[slot, cc, i : i + 1, :]
                 )
 
-    for cc in range(per):
+    for cc in range(units):
         for d in range(1, grid_size):
             for copy in z_copy(cc, d):
                 copy.wait_send()
@@ -503,6 +521,9 @@
 def collect(coded, scales, takes, grid_size, basis_size, owned, turns):
     per = CL // grid_size
     members = CL // owned
+    halves = math.gcd(owned, 2)
+    width = owned // halves
+    units = per * halves
     vmem = pl.BlockSpec(memory_space=pltpu.VMEM)
 
     def both(*lead):
@@ -516,18 +537,18 @@
         out_shape=jax.ShapeDtypeStruct((owned * TB, turns * per * TB), jnp.float32),
         in_specs=[vmem] * 3,
         out_specs=vmem,
-        scratch_shapes=both(grid_size - 1, per, CL)
-        + both(per, members, owned)
-        + both(basis_size - 1, per, owned)
-        + both(turns, per, owned)
-        + both(turns, per, owned)
+        scratch_shapes=both(grid_size - 1, units, members * width)
+        + both(units, members, width)
+        + both(basis_size - 1, units, width)
+        + both(turns, units, width)
+        + both(turns, units, width)
         + [
-            pltpu.SemaphoreType.DMA((grid_size - 1, per, 2)),
-            pltpu.SemaphoreType.DMA((grid_size - 1, per, 2)),
-            pltpu.SemaphoreType.DMA((basis_size - 1, per, 2)),
-            pltpu.SemaphoreType.DMA((basis_size - 1, per, 2)),
-            pltpu.SemaphoreType.DMA((turns, per, 2)),
-            pltpu.SemaphoreType.DMA((turns, per, 2)),
+            pltpu.SemaphoreType.DMA((grid_size - 1, units, 2)),
+            pltpu.SemaphoreType.DMA((grid_size - 1, units, 2)),
+            pltpu.SemaphoreType.DMA((basis_size - 1, units, 2)),
+            pltpu.SemaphoreType.DMA((basis_size - 1, units, 2)),
+            pltpu.SemaphoreType.DMA((turns, units, 2)),
+            pltpu.SemaphoreType.DMA((turns, units, 2)),
         ],
         compiler_params=pltpu.CompilerParams(
             collective_id=0, has_side_effects=True, vmem_limit_bytes=48 * 1024 * 1024
@@ -580,7 +601,8 @@
     packed = pack_density(columns, density)
     dens = fetch_density(slots, packed, grid_size, basis_size, owned_blocks)
     coded, scales = region_exchange(
-        block_lists % CL, counts.reshape(1), basis_values, weighted, boys, dens, coup, grid_size
+        block_lists % CL, counts.reshape(1), basis_values, weighted, boys, dens, coup, grid_size,
+        owned_blocks,
     )
     back = (me_basis - jnp.arange(basis_size, dtype=jnp.int32)) % basis_size
     begins = firsts[back]

time: 191 us -> 187 us (0.979)
  Pallas kernels: 161 us -> 156 us
    pallas_call x1, Pallas kernels: 83.5 us -> 74 us  [collect(): pl.pallas_call(functools.partial(collect_kernel, grid_size, basis_size, o...]
    pallas_call x1, Pallas kernels: 21.7 us -> 26.3 us  [region_exchange(): pl.pallas_call(functools.partial(batch_kernel, per, owned), grid_spec=plt...]
where the time goes in v2:
time: 187 us; the launch traced here: 186 us
  Pallas kernels  156 us (83%)
  local copies, waits for them, and re-layouts  12.8 us (7%)
  other arithmetic  11.3 us (6%)
  starting transfers between devices  4.53 us (2%)
    pallas_call x1, Pallas kernels, collect(): pl.pallas_call(functools.partial(collect_kernel, grid_size, basis_size, o...  74 us
    pallas_call x1, Pallas kernels, fetch_density(): pl.pallas_call(functools.partial(fetch_kernel, grid_size, basis_size, own...  52 us
    pallas_call x1, Pallas kernels, region_exchange(): pl.pallas_call(functools.partial(batch_kernel, per, owned), grid_spec=plt...  26.3 us
    unnamed x14, local copies, waits for them, and re-layouts  5.26 us
    all_to_all x1, starting transfers between devices, body(): lax.all_to_all(jnp.broadcast_to(first, (basis_size, 1)), 'basis', split_a...  4.53 us
    convert_element_type x1, other arithmetic, body(): weighted = (basis_values * scaled[:, :, None]).astype(jnp.bfloat16)  4 us
    pallas_call x1, Pallas kernels, pack_density(): pl.pallas_call(pack_kernel, in_specs=[pl.BlockSpec(memory_space=pltpu.SME...  3.94 us
  transfers between devices with their start and end apart: 1, of which 0 were waited for; matrix products, arithmetic and copies ran while one was open for 8% of the time, Pallas kernels for 0%

profile of v2, /device:TPU:27, one launch (start us, length us, event | category | flops | bytes accessed | tf_op | source)
XLA Modules:
  0.0 185.7 jit_solution(13343995883304926732)
XLA Ops:
  0.0 0.0 copy-start
  0.0 0.8 copy.67
  0.8 0.1 eq.47
  0.9 0.1 fusion.2
  1.0 0.6 slice.8
  1.6 1.4 fusion.22
  3.0 1.3 broadcast_in_dim.26
  4.3 4.5 %all-to-all-start = ((s32[8,1,1]{2,1,0:T(1,128)}), s32[8,1,1]{2,1,0:T(1,128)S(1)}, u32[]{:S(2)}, u32[]{:S(2)}) async-start(s32[8,1,1]{2,1,0:T(1,128)} %broadcast_in_dim.26), calls=%async_computation | async-start | bytes 8192 | tf_op jit(solution)/shard_map/all_to_all | solution.py:583
  8.8 0.7 and_select_fusion.1
  9.6 0.1 iota_add_fusion
  9.7 1.5 copy.80
  11.2 2.8 %gather_fusion.2 = f32[1024,3]{1,0:T(8,128)S(1)} fusion(f32[3,4096]{0,1:T(8,128)S(1)} %copy.80, s32[1024]{0:T(1024)S(1)} %broadcast_clamp_fusion), kind=kCustom, calls=%fused_computation.2 | custom fusion | bytes 28672 | tf_op jit(solution)/shard_map/gather | solution.py:42
  14.0 0.2 copy.81
  14.2 1.3 multiply_reduce_fusion
  15.4 0.0 copy-start.4
  15.5 0.0 copy-start.2
  15.5 1.9 %exponential_convert_fusion.coup_ref = bf16[8,8,128,128]{3,2,1,0:T(8,128)(2,1)} fusion(f32[8,8,128,128]{3,2,1,0:T(8,128)S(1)} %multiply_reduce_fusion), kind=kLoop, calls=%fused_computation.6 | loop fusion | flops 2097152 | bytes 6291456 | tf_op jit(solution)/shard_map/convert_element_type | solution.py:46
  17.4 0.1 reshape.276
  17.5 0.0 copy-done.4
  17.5 0.1 copy.75
  17.6 0.6 gather_fusion.1
  18.2 0.1 copy.76
  18.3 0.0 copy-done.2
  18.3 0.0 copy-done
  18.3 0.0 copy-start.3
  18.4 0.8 gather_fusion
  19.1 0.1 reshape.275
  19.2 0.1 copy.72
  19.3 0.1 copy.74
  20.1 0.2 multiply_reduce_fusion.1
  20.3 0.2 multiply_divide_fusion.boys_ref
  20.5 0.0 copy-done.3
  20.5 0.1 select_multiply_fusion
  20.6 4.0 %multiply_convert_fusion.weighted_ref = bf16[16,256,512]{2,1,0:T(8,128)(2,1)} fusion(bf16[16,256,512]{2,1,0:T(8,128)(2,1)} %values_ref.1, f32[16,256]{1,0:T(8,128)S(1)} %select_multiply_fusion), kind=kLoop, calls=%fused_computation.5 | loop fusion | flops 6291456 | bytes 8404992 | tf_op jit(solution)/shard_map/convert_element_type | solution.py:599
  24.6 0.0 all-to-all-done
  24.6 0.2 reduce
  24.8 0.7 gather_fusion.3
  25.5 0.7 add_select_fusion.1
  26.2 0.1 iota_compare_fusion.1
  26.2 0.1 fusion.6
  26.3 3.9 %pack_density.1.packed = bf16[8,2,512,128]{3,2,1,0:T(8,128)(2,1)} custom-call(s32[8,2]{1,0:T(8,128)} %get-tuple-element.12.column_ref, bf16[512,4096]{1,0:T(8,128)(2,1)} %dens_ref.1), custom_call_target="tpu_custom_call" | custom-call | tf_op jit(solution)/shard_map/pack_density/pallas_call | solution.py:69
  30.3 0.0 copy-start.1
  30.3 1.6 copy-done.1
  31.9 52.0 %fetch_density.1.dens_ref = bf16[4,2,8,128,128]{4,3,2,1,0:T(8,128)(2,1)S(1)} custom-call(s32[8]{0:T(128)S(1)} %get-tuple-element.13.slot_ref, bf16[8,2,512,128]{3,2,1,0:T(8,128)(2,1)S(1)} %copy-done.1), custom_call_target="tpu_custom_call" | custom-call | tf_op jit(solution)/shard_map/fetch_density/pallas_call | solution.py:191
  83.9 0.1 and_convert_fusion
  83.9 26.3 %region_exchange.1 = (s16[4,4,4,128,128]{4,3,2,1,0:T(8,128)(2,1)S(1)}, f32[4,4,4,128]{3,2,1,0:T(4,128)S(1)}) custom-call(s32[16,4]{1,0:T(8,128)S(1)} %get-tuple-element.10.place_ref, s32[1]{0:T(128)} %bitcast.17.count_ref, bf16[16,256,512]{2,1,0:T(8,128)(2,1)} %values_ref.1, bf16[16,256,512]{2,1,0:T(8,128)(2,1)} %multiply_convert_fusion.weighted_ref, ...), custom_call_target="tpu_custom_call" | custom-call | tf_op jit(solution)/shard_map/region_exchange/pallas_call | solution.py:296
  110.2 0.1 broadcast_in_dim.27.takes
  110.3 74.0 %collect.1 = f32[512,1024]{1,0:T(8,128)S(1)} custom-call(s16[4,4,4,128,128]{4,3,2,1,0:T(8,128)(2,1)S(1)} %get-tuple-element.7.kq, f32[4,4,4,128]{3,2,1,0:T(4,128)S(1)} %get-tuple-element.8.ks, f32[8,2,4,4,128]{4,3,2,1,0:T(4,128)S(1)} %broadcast_in_dim.27.takes), custom_call_target="tpu_custom_call" | custom-call | tf_op jit(solution)/shard_map/collect/pallas_call | solution.py:535
  184.4 1.3 copy.93
  (12 shorter events, 0.1 us)
Async XLA Ops:
  0.0 18.3 %copy-start = (f32[32]{0:T(128)S(1)}, f32[32]{0:T(128)}, u32[]{:S(2)}) copy-start(f32[32]{0:T(128)} %param.17) | copy-start | bytes 388
  4.3 20.3 %all-to-all-start = ((s32[8,1,1]{2,1,0:T(1,128)}), s32[8,1,1]{2,1,0:T(1,128)S(1)}, u32[]{:S(2)}, u32[]{:S(2)}) async-start(s32[8,1,1]{2,1,0:T(1,128)} %broadcast_in_dim.26), calls=%async_computation | async-start | bytes 8192 | tf_op jit(solution)/shard_map/all_to_all | solution.py:583
  15.4 2.1 %copy-start.4 = (f32[3,32]{1,0:T(4,128)S(1)}, f32[3,32]{1,0:T(4,128)}, u32[]{:S(2)}) copy-start(f32[3,32]{1,0:T(4,128)} %param.16) | copy-start | bytes 1156
  15.5 2.9 %copy-start.2 = (bf16[16,3,256]{2,0,1:T(8,128)(2,1)S(1)}, bf16[16,3,256]{2,0,1:T(8,128)(2,1)}, u32[]{:S(2)}) copy-start(bf16[16,3,256]{2,0,1:T(8,128)(2,1)} %param.11) | copy-start | bytes 73732
  18.3 2.2 %copy-start.3 = (f32[16,256]{1,0:T(8,128)S(1)}, f32[16,256]{1,0:T(8,128)}, u32[]{:S(2)}) copy-start(f32[16,256]{1,0:T(8,128)} %param.10) | copy-start | bytes 49156
  30.3 1.6 copy-start.1
